TPU v7x, 128 devices: a whole 4x4x4 slice. The times are simulated.
128 devices in a mesh: space: 32 (over z, y_hi, x), sample: 4 (over y_lo, core).
Axes of the slice: x: 4, y: 4 (y_hi: 2, y_lo: 2; y = y_hi * 2 + y_lo), z: 4, core: 2. Of those that a mesh axis runs over, the one named last changes fastest.
Arguments:
- state_hat: float32 [20, 3, 256, 32, 128], P('sample', None, 'space'), may hold values from -2.4 to 2.4
- adjoint_hat: float32 [20, 3, 256, 32, 128], P('sample', None, 'space'), may hold values from -2.4 to 2.4
- objective_hat: float32 [20, 3, 256, 32, 128], P('sample', None, 'space'), may hold values from -6 to 6
- density: float32 [256, 32, 128], P('space'), may hold values from 0.05 to 1
- region: int32 [256, 32, 128], P('space'), may hold values from 0 to 3
Outputs:
- adjoint_residual: float32 [20, 3, 256, 32, 128], P('sample', None, 'space')
- density_gradient: float32 [256, 32, 128], P('space', 'sample')
All inputs are finite; a program needn't handle non-finite values.
Results may differ from a plain program's by a relative error of at most 0.00026.
Values sent between devices are 32-bit elements; how exact they have to be, the bound alone decides.
A program may use at most 128 MiB of HBM per device.

v0:
```python
import math
import jax
import jax.numpy as jnp
from jax import lax
from jax.sharding import PartitionSpec as P

NCOEF = 20
NT = 40
magnet_reluct = 0.95
iron_floor = 0.05
saturation = 1.0


def passed_along(array, axis, by):
    size = lax.axis_size(axis)
    pairs = [(i, i + by) for i in range(size) if 0 <= i + by < size]
    return lax.ppermute(array, axis, pairs)


def harmonic_table():
    sample_steps = jnp.arange(NT, dtype=jnp.int32).astype(jnp.float32)
    orders = (jnp.arange(NCOEF // 2, dtype=jnp.int32) + 1).astype(jnp.float32)
    angles = 2.0 * math.pi / NT * sample_steps[:, None] * orders[None, :]
    return jnp.stack([jnp.cos(angles), jnp.sin(angles)], axis=2).reshape(NT, NCOEF)


def forward_diff(potential, along):
    length = potential.shape[along]
    widths = [(0, 0)] * potential.ndim
    widths[along] = (0, 1)
    padded = jnp.pad(potential, widths)
    return lax.slice_in_dim(padded, 1, length + 1, axis=along) - potential


def backward_diff(potential, along):
    length = potential.shape[along]
    widths = [(0, 0)] * potential.ndim
    widths[along] = (1, 0)
    padded = jnp.pad(potential, widths)
    return lax.slice_in_dim(padded, 0, length, axis=along) - potential


def curl_field(potential, upper):
    x_step = jnp.concatenate([potential[:, :, 1:], upper], axis=2) - potential
    part_one, part_two, part_three = (potential[:, 0], potential[:, 1], potential[:, 2])
    flux_one = forward_diff(part_three, 2) - forward_diff(part_two, 3)
    flux_two = forward_diff(part_one, 3) - x_step[:, 2]
    flux_three = x_step[:, 1] - forward_diff(part_one, 2)
    return jnp.stack([flux_one, flux_two, flux_three], axis=1)


def curl_back(field_h, lower):
    x_step = jnp.concatenate([lower, field_h[:, 1:3, :-1]], axis=2) - field_h[:, 1:3]
    back_one = backward_diff(field_h[:, 1], 3) - backward_diff(field_h[:, 2], 2)
    back_two = x_step[:, 1] - backward_diff(field_h[:, 0], 3)
    back_three = backward_diff(field_h[:, 0], 2) - x_step[:, 0]
    return jnp.stack([back_one, back_two, back_three], axis=1)


def material(density, region):
    iron_share = jnp.where(region == 0, density**3, jnp.zeros_like(density))
    iron_slope = jnp.where(region == 0, 3.0 * density**2, jnp.zeros_like(density))
    base_reluct = jnp.where(
        region == 1, magnet_reluct * jnp.ones_like(density), jnp.ones_like(density)
    )
    return (iron_share, iron_slope, base_reluct)


def reluctivity(state_flux, adjoint_flux, base_reluct, iron_share):
    flux_square = jnp.sum(state_flux * state_flux, axis=1)
    flux_inner = jnp.sum(state_flux * adjoint_flux, axis=1)
    iron_curve = iron_floor + (1.0 - iron_floor) * flux_square / (flux_square + saturation)
    curve_slope = (1.0 - iron_floor) * saturation / (flux_square + saturation) ** 2
    reluct_now = base_reluct + iron_share * (iron_curve - 1.0)
    reluct_slope = iron_share * curve_slope
    field_h = (
        reluct_now[:, None] * adjoint_flux + (2.0 * reluct_slope * flux_inner)[:, None] * state_flux
    )
    return (field_h, iron_curve, flux_inner)


def local(state_hat, adjoint_hat, objective_hat, density, region):
    harm_table = harmonic_table()
    groups = lax.axis_size("sample")
    local_times = NT // groups
    planes = state_hat.shape[2]
    first_time = lax.axis_index("sample") * local_times
    own_rows = lax.dynamic_slice_in_dim(harm_table, first_time, local_times, 0)
    iron_share, iron_slope, base_reluct = material(density, region)
    columns = own_rows
    state_time = jnp.tensordot(
        columns,
        lax.all_gather(state_hat, "sample", axis=0, tiled=True),
        axes=1,
        precision=lax.Precision.HIGHEST,
    )
    adjoint_time = jnp.tensordot(
        columns,
        lax.all_gather(adjoint_hat, "sample", axis=0, tiled=True),
        axes=1,
        precision=lax.Precision.HIGHEST,
    )
    first_planes = jnp.concatenate([state_time[:, :, :1], adjoint_time[:, :, :1]], axis=1)
    upper = passed_along(first_planes, "space", -1)
    state_flux = curl_field(state_time, upper[:, :3])
    adjoint_flux = curl_field(adjoint_time, upper[:, 3:])
    field_h, iron_curve, flux_inner = reluctivity(state_flux, adjoint_flux, base_reluct, iron_share)
    lower = passed_along(field_h[:, 1:3, planes - 1 :], "space", 1)
    back_field = curl_back(field_h, lower)
    partial_terms = -(1.0 / NT) * jnp.sum(iron_slope * (iron_curve - 1.0) * flux_inner, axis=0)
    columns = own_rows
    summed = lax.psum_scatter(
        2.0 / NT * jnp.tensordot(columns.T, back_field, axes=1, precision=lax.Precision.HIGHEST),
        "sample",
        scatter_dimension=0,
        tiled=True,
    )
    density_gradient = lax.psum_scatter(partial_terms, "sample", scatter_dimension=1, tiled=True)
    adjoint_residual = objective_hat - summed
    return (adjoint_residual, density_gradient)


def solution(mesh):
    in_specs = (
        P("sample", None, "space", None, None),
        P("sample", None, "space", None, None),
        P("sample", None, "space", None, None),
        P("space", None, None),
        P("space", None, None),
    )
    out_specs = (P("sample", None, "space", None, None), P("space", "sample", None))
    return jax.shard_map(local, mesh=mesh, in_specs=in_specs, out_specs=out_specs, check_vma=False)
```

profile of v0, /device:TPU:1, one launch (start us, length us, event | category | flops | bytes accessed | tf_op | source)
XLA Modules:
  0.0 376.0 jit_solution(5956820325559077423)
XLA Ops:
  7.2 0.0 copy-start.11
  7.2 0.0 copy-start.12
  7.2 0.0 all-gather.3.cloned.1.call-start
  7.2 0.7 all-gather.3.cloned.1.call-update
  7.9 0.0 all-gather.5.cloned.1.call-start
  8.0 0.7 all-gather.5.cloned.1.call-update
  8.7 0.0 reduce-scatter.3.cloned.1.call-start
  8.7 0.2 multiply_cosine_fusion
  9.0 0.0 copy-done.11
  9.0 0.0 copy-done.12
  9.0 0.8 fusion.43
  9.8 80.5 %all-gather.3.cloned.1.call-done = f32[20,3,8,32,128]{4,3,2,1,0:T(8,128)} async-done(((f32[5,3,8,32,128]{4,3,2,1,0:T(8,128)}), f32[20,3,8,32,128]{4,3,2,1,0:T(8,128)}) %all-gather.3.cloned.1.call-update) | async-done | bytes 7864336 | tf_op jit(solution)/shard_map/all_gather | solution.py:93
  90.3 14.4 %fusion.2 = f32[10,3,8,32,128]{4,0,3,2,1:T(8,128)S(1)} fusion(f32[20,3,8,32,128]{4,3,2,1,0:T(8,128)} %all-gather.3.cloned.1.call-done, f32[40,20]{0,1:T(8,128)S(1)} %reshape.127, s32[]{:T(128)S(6)} %select_n.13), kind=kOutput, calls=%fused_computation.2 | convolution fusion | flops 235929600 | bytes 11799684 | tf_op jit(solution)/shard_map/dot_general | solution.py:91
  104.8 0.0 copy-start
  104.8 2.8 copy-done
  107.5 0.1 slice.149
  107.6 62.3 %all-gather.5.cloned.1.call-done = f32[20,3,8,32,128]{4,3,2,1,0:T(8,128)} async-done(((f32[5,3,8,32,128]{4,3,2,1,0:T(8,128)}), f32[20,3,8,32,128]{4,3,2,1,0:T(8,128)}) %all-gather.5.cloned.1.call-update) | async-done | bytes 7864336 | tf_op jit(solution)/shard_map/all_gather | solution.py:99
  169.9 14.4 %fusion = f32[10,3,8,32,128]{4,0,3,2,1:T(8,128)S(1)} fusion(f32[20,3,8,32,128]{4,3,2,1,0:T(8,128)} %all-gather.5.cloned.1.call-done, f32[40,20]{0,1:T(8,128)S(1)} %reshape.127, s32[]{:T(128)S(6)} %select_n.13), kind=kOutput, calls=%fused_computation | convolution fusion | flops 235929600 | bytes 11799684 | tf_op jit(solution)/shard_map/dot_general | solution.py:97
  184.4 0.1 slice.150
  184.4 0.1 pad_maximum_fusion.2
  184.5 0.3 copy.19
  184.9 1.3 collective-permute-start
  186.2 0.9 fusion.42
  187.0 2.2 slice-done
  189.2 0.7 slice-done.1
  189.9 2.8 slice_bitcast_fusion.13
  192.7 3.4 slice_bitcast_fusion.8
  196.1 13.5 %collective-permute-done = f32[10,6,1,32,128]{4,3,2,1,0:T(8,128)S(1)} collective-permute-done((f32[10,6,1,32,128]{4,3,2,1,0:T(8,128)S(1)}, f32[10,6,1,32,128]{4,3,2,1,0:T(8,128)S(1)}, u32[]{:S(2)}, u32[]{:S(2)}) %collective-permute-start) | collective-permute-done | bytes 983072 | tf_op jit(solution)/shard_map/ppermute | solution.py:17
  209.6 0.1 fusion.54
  209.7 0.3 copy.25
  210.0 1.2 copy.26
  211.2 0.0 slice-done.2
  211.2 0.0 slice-start.5
  211.2 3.8 %maximum_subtract_fusion = f32[10,3,8,32,128]{4,0,3,2,1:T(8,128)} fusion(f32[10,3,8,32,128]{4,0,3,2,1:T(8,128)S(1)} %bitcast.77, f32[10,3,1,32,128]{4,0,3,2,1:T(8,128)S(1)} %copy.25, f32[10,3,7,32,128]{4,0,3,2,1:T(8,128)S(1)} %slice-done.4), kind=kLoop, calls=%fused_computation.4 | loop fusion | flops 1966080 | bytes 11796480 | tf_op jit(solution)/shard_map/sub | solution.py:44
  215.0 0.4 slice-done.5
  215.4 6.8 %maximum_subtract_fusion.1 = f32[10,3,8,32,128]{4,0,3,2,1:T(8,128)} fusion(f32[10,3,8,32,128]{4,0,3,2,1:T(8,128)} %copy-done.1, f32[10,3,1,32,128]{4,0,3,2,1:T(8,128)} %copy.26, f32[10,3,7,32,128]{4,0,3,2,1:T(8,128)S(1)} %slice-done.5), kind=kLoop, calls=%fused_computation.6 | loop fusion | flops 1966080 | bytes 11796480 | tf_op jit(solution)/shard_map/sub | solution.py:44
  222.3 0.0 slice-start.7
  222.3 5.8 %fusion.33 = (f32[10,1,8,32,128]{4,0,3,2,1:T(8,128)S(1)}, f32[10,1,8,32,128]{4,0,3,2,1:T(8,128)S(1)}, f32[10,1,8,32,128]{4,0,3,2,1:T(8,128)S(1)}) fusion(f32[10,8,32,128]{3,0,2,1:T(8,128)} %get-tuple-element.20, f32[10,3,8,32,128]{4,0,3,2,1:T(8,128)S(1)} %copy-done.2, f32[10,8,32,128]{3,0,2,1:T(8,128)S(1)} %copy-done.6, f32[10,8,32,128]{3,0,2,1:T(8,128)} %get-tuple-element.21), kind=kLoop, calls=%fused_computation.52 | loop fusion | flops 2293760 | bytes 10485760 | tf_op jit(solution)/shard_map/stack | solution.py:49
  228.2 0.6 copy-done.3
  228.8 0.6 copy-done.4
  229.4 0.6 copy-done.5
  230.0 1.7 fusion.37
  231.7 2.0 multiply_reduce_fusion.1
  233.8 0.0 copy-done.8
  233.8 0.0 copy-done.9
  233.8 0.0 copy-done.10
  233.8 1.6 multiply_reduce_fusion.2
  235.4 1.1 multiply_add_fusion
  236.5 0.6 slice_bitcast_fusion.4
  237.1 0.3 slice.164
  237.4 3.1 collective-permute-start.1
  240.6 0.6 fusion.26
  241.2 10.5 %collective-permute-done.1 = f32[10,2,1,32,128]{4,0,3,2,1:T(8,128)S(1)} collective-permute-done((f32[10,2,1,32,128]{4,0,3,2,1:T(8,128)S(1)}, f32[10,2,1,32,128]{4,0,3,2,1:T(8,128)S(1)}, u32[]{:S(2)}, u32[]{:S(2)}) %collective-permute-start.1) | collective-permute-done | bytes 327712 | tf_op jit(solution)/shard_map/ppermute | solution.py:17
  251.7 0.6 slice_subtract_fusion
  252.3 0.7 fusion.41
  253.1 8.6 %broadcast_multiply_fusion = f32[20,3,8,32,128]{4,0,3,2,1:T(8,128)S(1)} fusion(f32[10,1,8,32,128]{4,0,3,2,1:T(8,128)S(1)} %get-tuple-element.18, f32[10,1,8,32,128]{4,0,3,2,1:T(8,128)S(1)} %get-tuple-element.17, f32[10,1,8,32,128]{4,0,3,2,1:T(8,128)S(1)} %fusion.26, f32[40,20]{0,1:T(8,128)S(1)} %reshape.127, s32[]{:T(128)S(6)} %select_n.13), kind=kOutput, calls=%fused_computation.17 | convolution fusion | flops 239861760 | bytes 11799684 | tf_op jit(solution)/shard_map/dot_general | solution.py:113
  261.7 4.5 %copy.22 = f32[20,3,8,32,128]{4,3,2,1,0:T(8,128)} copy(f32[20,3,8,32,128]{4,0,3,2,1:T(8,128)S(1)} %broadcast_multiply_fusion) | data formatting | bytes 15728640 | tf_op jit(solution)/shard_map/mul | solution.py:113
  266.2 0.0 reduce-scatter.3.cloned.1.call-update
  266.2 0.0 reduce-scatter.5.cloned.1.call-start
  266.3 0.7 broadcast_multiply_fusion.1
  267.0 0.0 reduce-scatter.5.cloned.1.call-update
  267.0 81.5 %reduce-scatter.3.cloned.1.call-done = f32[5,3,8,32,128]{4,3,2,1,0:T(8,128)} async-done(((f32[20,3,8,32,128]{4,3,2,1,0:T(8,128)}), f32[5,3,8,32,128]{4,3,2,1,0:T(8,128)}) %reduce-scatter.3.cloned.1.call-update) | async-done | bytes 1966096 | tf_op jit(solution)/shard_map/reduce_scatter | solution.py:112
  348.4 3.3 sub.107
  351.7 17.7 %reduce-scatter.5.cloned.1.call-done = f32[8,8,128]{2,1,0:T(8,128)} async-done(((f32[8,32,128]{2,1,0:T(8,128)}), f32[8,8,128]{2,1,0:T(8,128)}) %reduce-scatter.5.cloned.1.call-update) | async-done | bytes 32784 | tf_op jit(solution)/shard_map/reduce_scatter | solution.py:118
  (32 shorter events, 0.1 us)
Async XLA Ops:
  7.2 1.8 copy-start.11
  7.2 1.8 copy-start.12
  7.2 83.1 %all-gather.3.cloned.1.call-start = ((), (), s32[]{:S(2)}) async-start(), calls=%async_computation.2 | async-start | bytes 9830400 | tf_op jit(solution)/shard_map/all_gather | solution.py:93
  7.9 162.0 %all-gather.5.cloned.1.call-start = ((), (), s32[]{:S(2)}) async-start(), calls=%async_computation.3 | async-start | bytes 9830400 | tf_op jit(solution)/shard_map/all_gather | solution.py:99
  8.7 339.8 %reduce-scatter.3.cloned.1.call-start = ((), (), s32[]{:S(2)}) async-start(), calls=%async_computation.4 | async-start | bytes 9830400 | tf_op jit(solution)/shard_map/reduce_scatter | solution.py:112
  104.8 2.8 copy-start
  184.3 8.4 %copy-start.1 = (f32[10,3,8,32,128]{4,0,3,2,1:T(8,128)}, f32[10,3,8,32,128]{4,0,3,2,1:T(8,128)S(1)}, u32[]{:S(2)}) copy-start(f32[10,3,8,32,128]{4,0,3,2,1:T(8,128)S(1)} %fusion) | copy-start | bytes 11796484
  184.9 24.8 %collective-permute-start = (f32[10,6,1,32,128]{4,3,2,1,0:T(8,128)S(1)}, f32[10,6,1,32,128]{4,3,2,1,0:T(8,128)S(1)}, u32[]{:S(2)}, u32[]{:S(2)}) collective-permute-start(f32[10,6,1,32,128]{4,3,2,1,0:T(8,128)S(1)} %copy.19), channel_id=1, source_target_pairs={{4,0},{8,4},{12,8},{16,12},{20,16},{24,20},{28,24},{32,28},{36,32}... | collective-permute-start | bytes 2949128 | tf_op jit(solution)/shard_map/ppermute | solution.py:17
  187.0 2.2 slice-start
  187.0 2.9 slice-start.1
  189.9 21.3 %slice-start.2 = ((s8[6291456]{0:T(1024)(128)(4,1)}), s8[2097152]{0:T(1024)(128)(4,1)S(1)}, s32[]{:S(2)}) async-start(s8[6291456]{0:T(1024)(128)(4,1)} %bitcast.76), calls=%async_computation.8 | async-start | bytes 4194304
  192.7 18.5 %slice-start.3 = ((s8[6291456]{0:T(1024)(128)(4,1)}), s8[4194304]{0:T(1024)(128)(4,1)S(1)}, s32[]{:S(2)}) async-start(s8[6291456]{0:T(1024)(128)(4,1)} %bitcast.76), calls=%async_computation.9 | async-start | bytes 8388608
  192.7 18.5 %slice-start.4 = ((f32[10,3,8,32,128]{4,0,3,2,1:T(8,128)}), f32[10,3,7,32,128]{4,0,3,2,1:T(8,128)S(1)}, s32[]{:S(2)}) async-start(f32[10,3,8,32,128]{4,0,3,2,1:T(8,128)} %copy-done), calls=%async_computation.10 | async-start | bytes 11010048 | tf_op jit(solution)/shard_map/slice | solution.py:44
  211.2 4.2 %slice-start.5 = ((f32[10,3,8,32,128]{4,0,3,2,1:T(8,128)}), f32[10,3,7,32,128]{4,0,3,2,1:T(8,128)S(1)}, s32[]{:S(2)}) async-start(f32[10,3,8,32,128]{4,0,3,2,1:T(8,128)} %copy-done.1), calls=%async_computation.11 | async-start | bytes 11010048 | tf_op jit(solution)/shard_map/slice | solution.py:44
  215.4 6.8 %copy-start.2 = (f32[10,3,8,32,128]{4,0,3,2,1:T(8,128)S(1)}, f32[10,3,8,32,128]{4,0,3,2,1:T(8,128)}, u32[]{:S(2)}) copy-start(f32[10,3,8,32,128]{4,0,3,2,1:T(8,128)} %maximum_subtract_fusion) | copy-start | bytes 11796484
  215.4 6.8 %copy-start.6 = (f32[10,8,32,128]{3,0,2,1:T(8,128)S(1)}, f32[10,8,32,128]{3,0,2,1:T(8,128)}, u32[]{:S(2)}) copy-start(f32[10,8,32,128]{3,0,2,1:T(8,128)} %get-tuple-element.19) | copy-start | bytes 3932164
  222.3 5.9 %slice-start.6 = ((s8[6291456]{0:T(1024)(128)(4,1)}), s8[4194304]{0:T(1024)(128)(4,1)S(1)}, s32[]{:S(2)}) async-start(s8[6291456]{0:T(1024)(128)(4,1)} %bitcast.78), calls=%async_computation.12 | async-start | bytes 8388608
  222.3 5.9 %slice-start.7 = ((s8[6291456]{0:T(1024)(128)(4,1)}), s8[2097152]{0:T(1024)(128)(4,1)S(1)}, s32[]{:S(2)}) async-start(s8[6291456]{0:T(1024)(128)(4,1)} %bitcast.78), calls=%async_computation.13 | async-start | bytes 4194304
  222.3 6.5 %copy-start.3 = (f32[10,8,32,128]{3,0,2,1:T(8,128)S(1)}, f32[10,8,32,128]{3,0,2,1:T(8,128)}, u32[]{:S(2)}) copy-start(f32[10,8,32,128]{3,0,2,1:T(8,128)} %get-tuple-element.22) | copy-start | bytes 3932164
  222.3 7.1 %copy-start.4 = (f32[10,8,32,128]{3,0,2,1:T(8,128)S(1)}, f32[10,8,32,128]{3,0,2,1:T(8,128)}, u32[]{:S(2)}) copy-start(f32[10,8,32,128]{3,0,2,1:T(8,128)} %get-tuple-element.23) | copy-start | bytes 3932164
  222.3 7.7 %copy-start.5 = (f32[10,8,32,128]{3,0,2,1:T(8,128)S(1)}, f32[10,8,32,128]{3,0,2,1:T(8,128)}, u32[]{:S(2)}) copy-start(f32[10,8,32,128]{3,0,2,1:T(8,128)} %get-tuple-element.24) | copy-start | bytes 3932164
  231.7 2.1 copy-start.8
  231.7 2.1 copy-start.9
  231.7 2.1 copy-start.10
  237.4 14.3 %collective-permute-start.1 = (f32[10,2,1,32,128]{4,0,3,2,1:T(8,128)S(1)}, f32[10,2,1,32,128]{4,0,3,2,1:T(8,128)S(1)}, u32[]{:S(2)}, u32[]{:S(2)}) collective-permute-start(f32[10,2,1,32,128]{4,0,3,2,1:T(8,128)S(1)} %slice.163), channel_id=1, source_target_pairs={{0,4},{4,8},{8,12},{12,16},{16,20},{20,24},{24,28},{28,32},{32,36}... | collective-permute-start | bytes 983048 | tf_op jit(solution)/shard_map/ppermute | solution.py:17
  266.2 82.2 %copy-start.7 = (f32[5,3,8,32,128]{4,3,2,1,0:T(8,128)S(1)}, f32[5,3,8,32,128]{4,3,2,1,0:T(8,128)}, u32[]{:S(2)}) copy-start(f32[5,3,8,32,128]{4,3,2,1,0:T(8,128)} %param.7) | copy-start | bytes 5898244
  266.2 103.2 %reduce-scatter.5.cloned.1.call-start = ((), (), s32[]{:S(2)}) async-start(), calls=%async_computation.5 | async-start | bytes 163840 | tf_op jit(solution)/shard_map/reduce_scatter | solution.py:118
Sparse Core Ops, SparseCore 0:
  9.7 80.6 all-gather.2
  92.0 77.8 all-gather.4
  266.4 82.0 reduce-scatter.2
  351.2 18.1 reduce-scatter.4
where the time goes:
time: 376 us
  waiting for transfers between devices  268 us (71%)
  matrix products  37.5 us (10%)
  other arithmetic  30.8 us (8%)
  local copies, waits for them, and re-layouts  21.4 us (6%)
  between operations  14.1 us (4%)
  starting transfers between devices  4.57 us (1%)
    reduce_scatter x1, waiting for transfers between devices, local(): lax.psum_scatter(2.0 / NT * jnp.tensordot(columns.T, back_field, axes=1,...  81.5 us
    all_gather x1, waiting for transfers between devices, local(): lax.all_gather(state_hat, 'sample', axis=0, tiled=True)  80.5 us
    all_gather x1, waiting for transfers between devices, local(): lax.all_gather(adjoint_hat, 'sample', axis=0, tiled=True)  62.3 us
    ppermute x2, waiting for transfers between devices, passed_along(): return lax.ppermute(array, axis, pairs)  24.1 us
    reduce_scatter x1, waiting for transfers between devices, local(): lax.psum_scatter(partial_terms, 'sample', scatter_dimension=1, tiled=True)  17.7 us
    dot_general x1, matrix products, local(): jnp.tensordot(columns, lax.all_gather(state_hat, 'sample', axis=0, tiled=...  14.4 us
    dot_general x1, matrix products, local(): jnp.tensordot(columns, lax.all_gather(adjoint_hat, 'sample', axis=0, tile...  14.4 us
    sub x2, other arithmetic, curl_field(): x_step = jnp.concatenate([potential[:, :, 1:], upper], axis=2) - potential  10.7 us
  transfers between devices with their start and end apart: 6, of which 6 were waited for; matrix products, arithmetic and copies ran while one was open for 7% of the time, Pallas kernels for 0%

commit v1 on v0

--- a/solution.py
+++ b/solution.py
@@ -90,7 +90,9 @@
     columns = own_rows
     state_time = jnp.tensordot(
         columns,
-        lax.all_gather(state_hat, "sample", axis=0, tiled=True),
+        jnp.concatenate(
+            lax.all_to_all(jnp.stack([state_hat] * lax.axis_size("sample")), "sample", 0, 0), axis=0
+        ),
         axes=1,
         precision=lax.Precision.HIGHEST,
     )

time: 376 us -> 411 us (1.093); the launches traced: 376 us -> 405 us
  other arithmetic: 30.8 us -> 43 us
  starting transfers between devices: 4.57 us -> 11.9 us
  waiting for transfers between devices: 268 us -> 274 us
    all_to_all x0 -> x1, waiting for transfers between devices: none -> 149 us  [local(): lax.all_to_all(jnp.stack([state_hat] * lax.axis_size('sample')), 'sample'...]
    all_gather x1 -> x0, waiting for transfers between devices: 80.5 us -> none  [local(): lax.all_gather(state_hat, 'sample', axis=0, tiled=True)]
    all_gather x1, waiting for transfers between devices: 62.3 us -> 0.02 us  [local(): lax.all_gather(adjoint_hat, 'sample', axis=0, tiled=True)]
    another operation x2, other arithmetic: 7.55 us -> 19.9 us  [curl_field(): return jnp.stack([flux_one, flux_two, flux_three], axis=1)]
    all_to_all x0 -> x1, starting transfers between devices: none -> 7.05 us  [local(): lax.all_to_all(jnp.stack([state_hat] * lax.axis_size('sample')), 'sample'...]
    another operation x0 -> x1, local copies, waits for them, and re-layouts: none -> 4.16 us  [local(): jnp.stack([state_hat] * lax.axis_size('sample'))]
    unnamed x40 -> x42, local copies, waits for them, and re-layouts: 8.95 us -> 7.51 us
  transfers between devices with their start and end apart: 6 -> 6, of which waited for: 6 -> 5; matrix products, arithmetic and copies ran while one was open for 7% -> 8% of each run, Pallas kernels for 0% -> 0%
where the time goes in v1:
time: 411 us; the launch traced here: 405 us
  waiting for transfers between devices  274 us (67%)
  other arithmetic  43 us (10%)
  matrix products  37.8 us (9%)
  local copies, waits for them, and re-layouts  24.1 us (6%)
  between operations  14.1 us (3%)
  starting transfers between devices  11.9 us (3%)
    all_to_all x1, waiting for transfers between devices, local(): lax.all_to_all(jnp.stack([state_hat] * lax.axis_size('sample')), 'sample'...  149 us
    reduce_scatter x1, waiting for transfers between devices, local(): lax.psum_scatter(2.0 / NT * jnp.tensordot(columns.T, back_field, axes=1,...  84.3 us
    ppermute x2, waiting for transfers between devices, passed_along(): return lax.ppermute(array, axis, pairs)  22.5 us
    another operation x2, other arithmetic, curl_field(): return jnp.stack([flux_one, flux_two, flux_three], axis=1)  19.9 us
    reduce_scatter x1, waiting for transfers between devices, local(): lax.psum_scatter(partial_terms, 'sample', scatter_dimension=1, tiled=True)  17.9 us
    dot_general x1, matrix products, local(): jnp.tensordot(columns, lax.all_gather(adjoint_hat, 'sample', axis=0, tile...  14.8 us
    dot_general x1, matrix products, local(): jnp.tensordot(columns, jnp.concatenate(lax.all_to_all(jnp.stack([state_ha...  14.4 us
    sub x2, other arithmetic, curl_field(): x_step = jnp.concatenate([potential[:, :, 1:], upper], axis=2) - potential  10.7 us
  transfers between devices with their start and end apart: 6, of which 5 were waited for; matrix products, arithmetic and copies ran while one was open for 8% of the time, Pallas kernels for 0%

profile of v1, /device:TPU:1, one launch (start us, length us, event | category | flops | bytes accessed | tf_op | source)
XLA Modules:
  0.0 405.3 jit_solution(3140519439670424233)
XLA Ops:
  7.2 0.0 copy-start.7
  7.2 0.0 all-gather.2.cloned.1.call-start
  7.2 0.7 all-gather.2.cloned.1.call-update
  7.9 0.8 copy-done.7
  8.7 4.2 %stack.49 = f32[4,5,3,8,32,128]{5,4,3,2,1,0:T(8,128)} broadcast(f32[5,3,8,32,128]{4,3,2,1,0:T(8,128)S(1)} %copy-done.7), dimensions={1,2,3,4,5} | broadcast | bytes 9830400 | tf_op jit(solution)/shard_map/stack | solution.py:94
  12.9 7.1 %all-to-all-start = ((f32[4,5,3,8,32,128]{5,4,3,2,1,0:T(8,128)}), f32[4,5,3,8,32,128]{5,4,3,2,1,0:T(8,128)}, u32[]{:S(2)}, u32[]{:S(2)}) async-start(f32[4,5,3,8,32,128]{5,4,3,2,1,0:T(8,128)} %stack.49), calls=%async_computation | async-start | bytes 15728640 | tf_op jit(solution)/shard_map/all_to_all | solution.py:94
  19.9 0.0 reduce-scatter.3.cloned.1.call-start
  19.9 0.2 multiply_cosine_fusion
  20.2 0.8 fusion.43
  21.0 148.7 %all-to-all-done = f32[4,5,3,8,32,128]{5,4,3,2,1,0:T(8,128)} async-done(((f32[4,5,3,8,32,128]{5,4,3,2,1,0:T(8,128)}), f32[4,5,3,8,32,128]{5,4,3,2,1,0:T(8,128)}, u32[]{:S(2)}, u32[]{:S(2)}) %all-to-all-start) | async-done | bytes 7864352 | tf_op jit(solution)/shard_map/all_to_all | solution.py:94
  169.7 14.4 %fusion.2 = f32[10,3,8,32,128]{4,0,3,2,1:T(8,128)S(1)} fusion(f32[20,3,8,32,128]{4,3,2,1,0:T(8,128)} %bitcast.3, f32[40,20]{0,1:T(8,128)S(1)} %reshape.132, s32[]{:T(128)S(6)} %select_n.13), kind=kOutput, calls=%fused_computation.2 | convolution fusion | flops 235929600 | bytes 11799684 | tf_op jit(solution)/shard_map/dot_general | solution.py:91
  184.2 2.7 copy-done
  186.9 0.1 slice.149
  186.9 0.0 all-gather.2.cloned.1.call-done
  186.9 14.8 %fusion = f32[10,3,8,32,128]{4,0,3,2,1:T(8,128)S(1)} fusion(f32[20,3,8,32,128]{4,3,2,1,0:T(8,128)} %all-gather.2.cloned.1.call-done, f32[40,20]{0,1:T(8,128)S(1)} %reshape.132, s32[]{:T(128)S(6)} %select_n.13), kind=kOutput, calls=%fused_computation | convolution fusion | flops 235929600 | bytes 11799684 | tf_op jit(solution)/shard_map/dot_general | solution.py:99
  201.7 0.1 slice.150
  201.8 0.2 pad_maximum_fusion.2
  201.9 0.0 slice-start
  202.0 0.3 copy.19
  202.3 1.6 collective-permute-start
  203.8 0.7 fusion.42
  204.5 1.7 slice-done
  206.2 0.8 slice-done.1
  207.0 2.8 slice_bitcast_fusion.13
  209.8 0.0 copy-done.1
  209.8 3.4 slice_bitcast_fusion.8
  213.2 13.7 %collective-permute-done = f32[10,6,1,32,128]{4,3,2,1,0:T(8,128)S(1)} collective-permute-done((f32[10,6,1,32,128]{4,3,2,1,0:T(8,128)S(1)}, f32[10,6,1,32,128]{4,3,2,1,0:T(8,128)S(1)}, u32[]{:S(2)}, u32[]{:S(2)}) %collective-permute-start) | collective-permute-done | bytes 983072 | tf_op jit(solution)/shard_map/ppermute | solution.py:17
  226.9 0.1 fusion.54
  227.0 0.3 copy.25
  227.3 1.2 copy.26
  228.5 0.0 slice-done.2
  228.5 0.0 slice-done.4
  228.5 0.0 slice-start.5
  228.5 3.8 maximum_subtract_fusion
  232.3 0.4 slice-done.5
  232.7 6.8 %maximum_subtract_fusion.1 = f32[10,3,8,32,128]{4,0,3,2,1:T(8,128)} fusion(f32[10,3,8,32,128]{4,0,3,2,1:T(8,128)} %copy-done.1, f32[10,3,1,32,128]{4,0,3,2,1:T(8,128)} %copy.26, f32[10,3,7,32,128]{4,0,3,2,1:T(8,128)S(1)} %slice-done.5), kind=kLoop, calls=%fused_computation.6 | loop fusion | flops 1966080 | bytes 11796480 | tf_op jit(solution)/shard_map/sub | solution.py:44
  239.6 0.0 copy-done.6
  239.6 0.0 slice-start.7
  239.6 18.2 %fusion.33 = (f32[10,1,8,32,128]{4,0,3,2,1:T(8,128)S(1)}, f32[10,1,8,32,128]{4,0,3,2,1:T(8,128)S(1)}, f32[10,1,8,32,128]{4,0,3,2,1:T(8,128)S(1)}) fusion(f32[10,8,32,128]{3,0,2,1:T(8,128)} %get-tuple-element.20, f32[10,3,8,32,128]{4,0,3,2,1:T(8,128)S(1)} %copy-done.2, f32[10,8,32,128]{3,0,2,1:T(8,128)S(1)} %copy-done.6, f32[10,8,32,128]{3,0,2,1:T(8,128)} %get-tuple-element.21), kind=kLoop, calls=%fused_computation.52 | loop fusion | flops 2293760 | bytes 10485760 | tf_op jit(solution)/shard_map/stack | solution.py:49
  257.8 0.0 slice-done.6
  257.8 0.0 slice-done.7
  257.8 0.0 copy-done.3
  257.8 0.0 copy-done.4
  257.8 0.0 copy-done.5
  257.9 1.7 fusion.37
  259.6 2.0 multiply_reduce_fusion.1
  261.7 1.6 multiply_reduce_fusion.2
  263.3 1.1 multiply_add_fusion
  264.4 0.6 slice_bitcast_fusion.4
  265.0 0.3 slice.164
  265.3 3.3 collective-permute-start.1
  268.6 0.6 fusion.26
  269.2 8.8 %collective-permute-done.1 = f32[10,2,1,32,128]{4,0,3,2,1:T(8,128)S(1)} collective-permute-done((f32[10,2,1,32,128]{4,0,3,2,1:T(8,128)S(1)}, f32[10,2,1,32,128]{4,0,3,2,1:T(8,128)S(1)}, u32[]{:S(2)}, u32[]{:S(2)}) %collective-permute-start.1) | collective-permute-done | bytes 327712 | tf_op jit(solution)/shard_map/ppermute | solution.py:17
  278.0 0.6 slice_subtract_fusion
  278.6 0.7 fusion.41
  279.4 8.6 %broadcast_multiply_fusion = f32[20,3,8,32,128]{4,0,3,2,1:T(8,128)S(1)} fusion(f32[10,1,8,32,128]{4,0,3,2,1:T(8,128)S(1)} %get-tuple-element.18, f32[10,1,8,32,128]{4,0,3,2,1:T(8,128)S(1)} %get-tuple-element.17, f32[10,1,8,32,128]{4,0,3,2,1:T(8,128)S(1)} %fusion.26, f32[40,20]{0,1:T(8,128)S(1)} %reshape.132, s32[]{:T(128)S(6)} %select_n.13), kind=kOutput, calls=%fused_computation.17 | convolution fusion | flops 239861760 | bytes 11799684 | tf_op jit(solution)/shard_map/dot_general | solution.py:115
  288.0 4.5 %copy.22 = f32[20,3,8,32,128]{4,3,2,1,0:T(8,128)} copy(f32[20,3,8,32,128]{4,0,3,2,1:T(8,128)S(1)} %broadcast_multiply_fusion) | data formatting | bytes 15728640 | tf_op jit(solution)/shard_map/mul | solution.py:115
  292.5 0.0 reduce-scatter.3.cloned.1.call-update
  292.5 0.0 reduce-scatter.5.cloned.1.call-start
  292.6 0.7 broadcast_multiply_fusion.1
  293.3 0.0 reduce-scatter.5.cloned.1.call-update
  293.3 84.3 %reduce-scatter.3.cloned.1.call-done = f32[5,3,8,32,128]{4,3,2,1,0:T(8,128)} async-done(((f32[20,3,8,32,128]{4,3,2,1,0:T(8,128)}), f32[5,3,8,32,128]{4,3,2,1,0:T(8,128)}) %reduce-scatter.3.cloned.1.call-update) | async-done | bytes 1966096 | tf_op jit(solution)/shard_map/reduce_scatter | solution.py:114
  377.6 3.3 sub.107
  380.9 17.9 %reduce-scatter.5.cloned.1.call-done = f32[8,8,128]{2,1,0:T(8,128)} async-done(((f32[8,32,128]{2,1,0:T(8,128)}), f32[8,8,128]{2,1,0:T(8,128)}) %reduce-scatter.5.cloned.1.call-update) | async-done | bytes 32784 | tf_op jit(solution)/shard_map/reduce_scatter | solution.py:120
  (34 shorter events, 0.1 us)
Async XLA Ops:
  7.2 1.5 copy-start.7
  7.2 179.8 %all-gather.2.cloned.1.call-start = ((), (), s32[]{:S(2)}) async-start(), calls=%async_computation.3 | async-start | bytes 9830400 | tf_op jit(solution)/shard_map/all_gather | solution.py:101
  12.9 7.3 %copy-start.12 = (f32[8,32,128]{2,1,0:T(8,128)S(1)}, f32[8,32,128]{2,1,0:T(8,128)}, u32[]{:S(2)}) copy-start(f32[8,32,128]{2,1,0:T(8,128)} %param.8) | copy-start | bytes 393220
  12.9 7.3 %copy-start.13 = (s32[8,32,128]{2,1,0:T(8,128)S(1)}, s32[8,32,128]{2,1,0:T(8,128)}, u32[]{:S(2)}) copy-start(s32[8,32,128]{2,1,0:T(8,128)} %param.9) | copy-start | bytes 393220
  12.9 156.9 %all-to-all-start = ((f32[4,5,3,8,32,128]{5,4,3,2,1,0:T(8,128)}), f32[4,5,3,8,32,128]{5,4,3,2,1,0:T(8,128)}, u32[]{:S(2)}, u32[]{:S(2)}) async-start(f32[4,5,3,8,32,128]{5,4,3,2,1,0:T(8,128)} %stack.49), calls=%async_computation | async-start | bytes 15728640 | tf_op jit(solution)/shard_map/all_to_all | solution.py:94
  19.9 357.7 %reduce-scatter.3.cloned.1.call-start = ((), (), s32[]{:S(2)}) async-start(), calls=%async_computation.4 | async-start | bytes 9830400 | tf_op jit(solution)/shard_map/reduce_scatter | solution.py:114
  184.2 2.7 copy-start
  201.7 8.1 %copy-start.1 = (f32[10,3,8,32,128]{4,0,3,2,1:T(8,128)}, f32[10,3,8,32,128]{4,0,3,2,1:T(8,128)S(1)}, u32[]{:S(2)}) copy-start(f32[10,3,8,32,128]{4,0,3,2,1:T(8,128)S(1)} %fusion) | copy-start | bytes 11796484
  201.9 4.3 %slice-start = ((s8[6291456]{0:T(1024)(128)(4,1)}), s8[4194304]{0:T(1024)(128)(4,1)S(1)}, s32[]{:S(2)}) async-start(s8[6291456]{0:T(1024)(128)(4,1)} %bitcast.75), calls=%async_computation.6 | async-start | bytes 8388608
  202.3 24.6 %collective-permute-start = (f32[10,6,1,32,128]{4,3,2,1,0:T(8,128)S(1)}, f32[10,6,1,32,128]{4,3,2,1,0:T(8,128)S(1)}, u32[]{:S(2)}, u32[]{:S(2)}) collective-permute-start(f32[10,6,1,32,128]{4,3,2,1,0:T(8,128)S(1)} %copy.19), channel_id=1, source_target_pairs={{4,0},{8,4},{12,8},{16,12},{20,16},{24,20},{28,24},{32,28},{36,32}... | collective-permute-start | bytes 2949128 | tf_op jit(solution)/shard_map/ppermute | solution.py:17
  204.5 2.5 slice-start.1
  209.8 18.7 %slice-start.2 = ((s8[6291456]{0:T(1024)(128)(4,1)}), s8[4194304]{0:T(1024)(128)(4,1)S(1)}, s32[]{:S(2)}) async-start(s8[6291456]{0:T(1024)(128)(4,1)} %bitcast.77), calls=%async_computation.8 | async-start | bytes 8388608
  209.8 18.7 %slice-start.3 = ((s8[6291456]{0:T(1024)(128)(4,1)}), s8[2097152]{0:T(1024)(128)(4,1)S(1)}, s32[]{:S(2)}) async-start(s8[6291456]{0:T(1024)(128)(4,1)} %bitcast.77), calls=%async_computation.9 | async-start | bytes 4194304
  209.8 18.7 %slice-start.4 = ((f32[10,3,8,32,128]{4,0,3,2,1:T(8,128)}), f32[10,3,7,32,128]{4,0,3,2,1:T(8,128)S(1)}, s32[]{:S(2)}) async-start(f32[10,3,8,32,128]{4,0,3,2,1:T(8,128)} %copy-done), calls=%async_computation.10 | async-start | bytes 11010048 | tf_op jit(solution)/shard_map/slice | solution.py:44
  228.5 4.2 %slice-start.5 = ((f32[10,3,8,32,128]{4,0,3,2,1:T(8,128)}), f32[10,3,7,32,128]{4,0,3,2,1:T(8,128)S(1)}, s32[]{:S(2)}) async-start(f32[10,3,8,32,128]{4,0,3,2,1:T(8,128)} %copy-done.1), calls=%async_computation.11 | async-start | bytes 11010048 | tf_op jit(solution)/shard_map/slice | solution.py:44
  232.7 6.8 %copy-start.2 = (f32[10,3,8,32,128]{4,0,3,2,1:T(8,128)S(1)}, f32[10,3,8,32,128]{4,0,3,2,1:T(8,128)}, u32[]{:S(2)}) copy-start(f32[10,3,8,32,128]{4,0,3,2,1:T(8,128)} %maximum_subtract_fusion) | copy-start | bytes 11796484
  232.7 6.8 %copy-start.6 = (f32[10,8,32,128]{3,0,2,1:T(8,128)S(1)}, f32[10,8,32,128]{3,0,2,1:T(8,128)}, u32[]{:S(2)}) copy-start(f32[10,8,32,128]{3,0,2,1:T(8,128)} %get-tuple-element.19) | copy-start | bytes 3932164
  239.5 18.3 %slice-start.6 = ((s8[6291456]{0:T(1024)(128)(4,1)}), s8[4194304]{0:T(1024)(128)(4,1)S(1)}, s32[]{:S(2)}) async-start(s8[6291456]{0:T(1024)(128)(4,1)} %bitcast.79), calls=%async_computation.12 | async-start | bytes 8388608
  239.6 18.3 %slice-start.7 = ((s8[6291456]{0:T(1024)(128)(4,1)}), s8[2097152]{0:T(1024)(128)(4,1)S(1)}, s32[]{:S(2)}) async-start(s8[6291456]{0:T(1024)(128)(4,1)} %bitcast.79), calls=%async_computation.13 | async-start | bytes 4194304
  239.6 18.3 %copy-start.3 = (f32[10,8,32,128]{3,0,2,1:T(8,128)S(1)}, f32[10,8,32,128]{3,0,2,1:T(8,128)}, u32[]{:S(2)}) copy-start(f32[10,8,32,128]{3,0,2,1:T(8,128)} %get-tuple-element.22) | copy-start | bytes 3932164
  239.6 18.3 %copy-start.4 = (f32[10,8,32,128]{3,0,2,1:T(8,128)S(1)}, f32[10,8,32,128]{3,0,2,1:T(8,128)}, u32[]{:S(2)}) copy-start(f32[10,8,32,128]{3,0,2,1:T(8,128)} %get-tuple-element.23) | copy-start | bytes 3932164
  239.6 18.3 %copy-start.5 = (f32[10,8,32,128]{3,0,2,1:T(8,128)S(1)}, f32[10,8,32,128]{3,0,2,1:T(8,128)}, u32[]{:S(2)}) copy-start(f32[10,8,32,128]{3,0,2,1:T(8,128)} %get-tuple-element.24) | copy-start | bytes 3932164
  259.6 2.1 copy-start.9
  259.6 2.1 copy-start.10
  259.6 2.1 copy-start.11
  265.3 12.7 %collective-permute-start.1 = (f32[10,2,1,32,128]{4,0,3,2,1:T(8,128)S(1)}, f32[10,2,1,32,128]{4,0,3,2,1:T(8,128)S(1)}, u32[]{:S(2)}, u32[]{:S(2)}) collective-permute-start(f32[10,2,1,32,128]{4,0,3,2,1:T(8,128)S(1)} %slice.163), channel_id=1, source_target_pairs={{0,4},{4,8},{8,12},{12,16},{16,20},{20,24},{24,28},{28,32},{32,36}... | collective-permute-start | bytes 983048 | tf_op jit(solution)/shard_map/ppermute | solution.py:17
  292.5 85.1 %copy-start.8 = (f32[5,3,8,32,128]{4,3,2,1,0:T(8,128)S(1)}, f32[5,3,8,32,128]{4,3,2,1,0:T(8,128)}, u32[]{:S(2)}) copy-start(f32[5,3,8,32,128]{4,3,2,1,0:T(8,128)} %param.7) | copy-start | bytes 5898244
  292.5 106.2 %reduce-scatter.5.cloned.1.call-start = ((), (), s32[]{:S(2)}) async-start(), calls=%async_computation.5 | async-start | bytes 163840 | tf_op jit(solution)/shard_map/reduce_scatter | solution.py:120
Sparse Core Ops, SparseCore 0:
  9.6 145.0 all-gather.1
  292.7 84.9 reduce-scatter.2
  380.6 18.1 reduce-scatter.4
